TPU v7x, 32 devices: a whole 2x2x4 slice. The times are simulated.
32 devices in a mesh: group: 2 (over x), row: 16 (over z, y, core).
Axes of the slice: x: 2, y: 2, z: 4, core: 2. Of those that a mesh axis runs over, the one named last changes fastest.
Arguments:
- alignment: bfloat16 [256, 128, 256], P(('group', 'row')), parts along dimension 0, may hold values from -6 to 6
- pair_rep: bfloat16 [256, 128, 128], P(('group', 'row')), parts along dimension 0, may hold values from -6 to 6
- alignment_norm_gain: float32 [256], replicated, may hold values from 0.5 to 1.5
- alignment_norm_offset: float32 [256], replicated, may hold values from -3 to 3
- left_projection_weight: bfloat16 [256, 32], replicated, may hold values from -0.375 to 0.375
- right_projection_weight: bfloat16 [256, 32], replicated, may hold values from -0.375 to 0.375
- outer_weight: bfloat16 [1024, 128], replicated, may hold values from -0.75 to 0.75
- outer_bias: float32 [128], replicated, may hold values from -3 to 3
- pair_gain: float32 [128], replicated, may hold values from 0.5 to 1.5
- pair_shift: float32 [128], replicated, may hold values from -3 to 3
- up_weight: bfloat16 [128, 512], replicated, may hold values from -0.5 to 0.5
- up_bias: float32 [512], replicated, may hold values from -3 to 3
- down_weight: bfloat16 [512, 128], replicated, may hold values from -0.25 to 0.25
- down_bias: float32 [128], replicated, may hold values from -3 to 3
Outputs:
- pair_out: bfloat16 [256, 128, 128], P(('group', 'row')), parts along dimension 0
There are 2 independent parts, one for each index of `group`. A program takes and returns all parts, laid end to end along the dimension named above; an argument that names none is the same for every part. Nothing has to cross between parts.
All inputs are finite; a program needn't handle non-finite values.
Results may differ from a plain program's by a relative error of at most 0.005.
Values may be sent and summed in bfloat16 or wider, within the bound.
No kernel may reach another device: no remote copies, remote signals or barrier semaphores. Data moves between devices by JAX's collectives and lax.ppermute only.
A program may use at most 128 MiB of HBM per device.

v0:
```python
import functools

import jax
import jax.numpy as jnp
from jax import lax
from jax.experimental import pallas as pl
from jax.experimental.pallas import tpu as pltpu
from jax.sharding import PartitionSpec as P


epsilon = 1e-05
LANES = 128
CORES = 2


VMEM = pl.BlockSpec(memory_space=pltpu.VMEM)
SMEM = pl.BlockSpec(memory_space=pltpu.SMEM)
HBM = pl.BlockSpec(memory_space=pltpu.HBM)


def layer_norm(values, gain, shift):
    values = values.astype(jnp.float32)
    center = jnp.mean(values, axis=-1, keepdims=True)
    spread = jnp.mean(jnp.square(values - center), axis=-1, keepdims=True)
    return (values - center) * lax.rsqrt(spread + epsilon) * gain + shift


def pair_update(left_flat, right_flat, pair_tile, layer_params, proj_w):
    outer_weight, outer_bias, pair_gain, pair_shift, up_weight, up_bias, down_weight, down_bias = (
        layer_params
    )
    rows_i = left_flat.shape[0]
    rows_j = right_flat.shape[0]
    width = outer_weight.shape[1]
    seq_total = left_flat.shape[1] // proj_w
    left_rows = left_flat.reshape(rows_i, seq_total, proj_w)
    right_rows = right_flat.reshape(rows_j, seq_total, proj_w)
    outer_mean = jnp.einsum(
        "isc,jse->ijce", left_rows, right_rows, preferred_element_type=jnp.float32
    ) * (1.0 / seq_total)
    outer_mean = outer_mean.astype(jnp.bfloat16).reshape(rows_i * rows_j, proj_w * proj_w)
    summed = (
        pair_tile.reshape(rows_i * rows_j, width).astype(jnp.float32)
        + jnp.dot(outer_mean, outer_weight, preferred_element_type=jnp.float32)
        + outer_bias
    )
    normed = layer_norm(summed, pair_gain, pair_shift).astype(jnp.bfloat16)
    hidden = jax.nn.relu(
        jnp.dot(normed, up_weight, preferred_element_type=jnp.float32) + up_bias
    ).astype(jnp.bfloat16)
    result = summed + jnp.dot(hidden, down_weight, preferred_element_type=jnp.float32) + down_bias
    return result.astype(jnp.bfloat16).reshape(rows_i, rows_j, width)


def in_blocks(amount, builder):
    if amount > 256 and amount % 256 == 0:
        stacked = lax.map(
            lambda which_k: builder(which_k * 256, 256), jnp.arange(amount // 256, dtype=jnp.int32)
        )
        return stacked.reshape((amount,) + stacked.shape[2:])
    return builder(0, amount)


def plain_shards(alignment, pair_rep, align_gain, align_offset, left_weight, right_weight, *layer_params):
    proj_w = left_weight.shape[1]
    normed = layer_norm(alignment, align_gain, align_offset).astype(jnp.bfloat16)
    both = [
        jnp.einsum("src,cd->rsd", normed, weight, preferred_element_type=jnp.float32).astype(jnp.bfloat16)
        for weight in (left_weight, right_weight)
    ]
    left, right = [
        lax.all_to_all(x, "row", split_axis=0, concat_axis=1, tiled=True).reshape(
            x.shape[0] // lax.axis_size("row"), -1
        )
        for x in both
    ]
    pieces = lax.all_gather(right, "row", axis=0, tiled=True)

    def builder(start, amount):
        segment = lax.dynamic_slice_in_dim(pieces, start, amount, 0)
        pair_tile = lax.dynamic_slice_in_dim(pair_rep, start, amount, 1)
        return jnp.transpose(pair_update(left, segment, pair_tile, layer_params, proj_w), (1, 0, 2))

    columns = in_blocks(pieces.shape[0], builder)
    return lax.all_to_all(columns, "row", split_axis=0, concat_axis=1, tiled=True)


class Layout:
    def __init__(self, n, seq, residues, own_rows, proj_w):
        self.n, self.chips = n, n // CORES
        self.far = self.chips // 2
        self.seq, self.residues, self.rows, self.proj = seq, residues, own_rows, proj_w
        self.per = 16 // seq
        self.fold = LANES // proj_w
        self.chip_rows = CORES * own_rows
        self.left = proj_w * seq
        self.right = self.chip_rows // self.fold * seq
        self.pair = self.chip_rows * own_rows
        self.relayed = self.left + self.right

    def crosses(self, k):
        return k >= self.far and k % 2 == 0

    def right_at(self, k):
        return self.left + (self.right if self.crosses(k) else 0)

    def pair_at(self, k):
        return 0 if self.pair_only(k) else self.right_at(k) + self.right

    def pair_only(self, k):
        return k >= self.far and k % 2 == 1

    def total(self, k):
        return self.pair_at(k) + self.pair


def send_kernel(lay, place, x_ref, pair_ref, gain_ref, offset_ref, wl_ref, wr_ref, *rest):
    bufs, (norm_ref, left_ref) = rest[: lay.chips], rest[lay.chips :]
    seq, residues, proj, fold = lay.seq, lay.residues, lay.proj, lay.fold
    f32, bf16 = jnp.float32, jnp.bfloat16
    halves = norm_ref.shape[0]
    nt = (((1,), (1,)), ((), ()))
    x = x_ref[...].reshape(seq * residues, x_ref.shape[2])
    normed = layer_norm(x, gain_ref[...], offset_ref[...])
    for h in range(halves):
        norm_ref[h] = normed[:, h * LANES : (h + 1) * LANES]
    left = lax.dot_general(wl_ref[...], normed.astype(bf16), nt, preferred_element_type=f32)
    for s in range(seq):
        left_ref[s * proj : (s + 1) * proj, :] = left[:, s * residues : (s + 1) * residues]
    for tile in range(proj // lay.per):
        rows = jnp.concatenate(
            [left_ref[pl.ds(tile * lay.per + b, seq, stride=proj), :] for b in range(lay.per)], axis=0
        ).astype(bf16)
        for k, buf in enumerate(bufs):
            if not lay.pair_only(k):
                buf[tile * 16 : (tile + 1) * 16, :] = rows
    groups = residues // fold
    wr = wr_ref[...]
    zero = jnp.zeros_like(wr)
    right = None
    for g in range(fold):
        rows = jnp.concatenate(
            [
                jnp.concatenate(
                    [norm_ref[h, pl.ds(u * fold + g, seq, stride=residues), :] for u in range(groups)], axis=0
                )
                for h in range(halves)
            ],
            axis=1,
        ).astype(bf16)
        weight = jnp.concatenate([wr if h == g else zero for h in range(fold)], axis=0)
        part = lax.dot_general(rows, weight, nt, preferred_element_type=f32)
        right = part if right is None else right + part
    left_ref[...] = right

    def right_of(k):
        at = pl.multiple_of(lax.bitwise_xor(place[0], k) * lay.right, lay.right)
        return left_ref[pl.ds(at, lay.right), :].astype(bf16)

    for k, buf in enumerate(bufs):
        if not lay.pair_only(k):
            at = lay.right_at(k)
            buf[at : at + lay.right, :] = right_of(k)
        if lay.crosses(k):
            buf[lay.left : lay.left + lay.right, :] = right_of(k ^ 1)
        at = pl.multiple_of(lax.bitwise_xor(place[0], k) * lay.chip_rows, lay.chip_rows)
        tile = pair_ref[:, pl.ds(at, lay.chip_rows), :].astype(f32)
        tile = jnp.swapaxes(tile, 0, 1).reshape(lay.pair, LANES)
        at = lay.pair_at(k)
        buf[at : at + lay.pair, :] = tile.astype(bf16)


def update_kernel(lay, outers, pairs, place, *rest):
    count = max([b for b, _ in outers] + [b for b, _, _ in pairs]) + 1
    bufs = rest[:count]
    (ow_ref, ob_ref, pg_ref, ps_ref, uw_ref, ub_ref, dw_ref, db_ref, out_ref, outer_ref, pair_ref) = rest[count:]
    seq, residues, proj, rows_j, fold, per = lay.seq, lay.residues, lay.proj, lay.rows, lay.fold, lay.per
    f32, bf16 = jnp.float32, jnp.bfloat16
    chip, core = place[0], place[1]
    groups = rows_j // fold
    own = pl.multiple_of(core * (groups * seq), groups * seq)
    spread = []
    for b in range(per):
        rows = []
        for m, at in outers:
            got = bufs[m][pl.ds(at + own, groups * seq), :].astype(f32)
            got = jnp.concatenate([got[u * seq : (u + 1) * seq] for u in range(groups)], axis=1)
            zero = jnp.zeros_like(got)
            rows += [got if h == b else zero for h in range(per)]
        spread.append(jnp.concatenate(rows, axis=0).T.astype(bf16))
    right = jnp.concatenate(spread, axis=0)
    wide = 2
    scale = 1.0 / (seq * lay.n)
    for tile in range(0, proj // per, wide):
        left = jnp.concatenate(
            [
                jnp.concatenate([bufs[m][t * 16 : (t + 1) * 16, :] for m, _ in outers], axis=0)
                for t in range(tile, tile + wide)
            ],
            axis=1,
        )
        x = (jnp.dot(right, left, preferred_element_type=f32) * scale).astype(bf16)
        for b in range(per):
            for w in range(wide):
                c = (tile + w) * per + b
                for j in range(rows_j):
                    at = (b * rows_j + j) * proj
                    outer_ref[c * proj : (c + 1) * proj, j * residues : (j + 1) * residues] = x[
                        at : at + proj, w * residues : (w + 1) * residues
                    ]
    own = pl.multiple_of(core * (rows_j * rows_j), rows_j * rows_j)
    for m, at, k in pairs:
        sender = lax.bitwise_xor(chip * CORES + core, k)
        got = bufs[m][pl.ds(at + own, rows_j * rows_j), :].astype(f32)
        for j in range(rows_j):
            pair_ref[j, pl.ds(pl.multiple_of(sender * rows_j, rows_j), rows_j), :] = got[j * rows_j : (j + 1) * rows_j]
    added = lax.dot_general(ow_ref[...], outer_ref[...], (((0,), (0,)), ((), ())), preferred_element_type=f32)
    step = 4
    for j0 in range(0, rows_j, step):
        summed = jnp.concatenate(
            [added[:, j * residues : (j + 1) * residues].T + pair_ref[j] for j in range(j0, j0 + step)], axis=0
        )
        summed = summed + ob_ref[...]
        normed = layer_norm(summed, pg_ref[...], ps_ref[...]).astype(bf16)
        hidden = jnp.dot(normed, uw_ref[...], preferred_element_type=f32) + ub_ref[...]
        hidden = jnp.maximum(hidden, 0.0).astype(bf16)
        result = summed + jnp.dot(hidden, dw_ref[...], preferred_element_type=f32) + db_ref[...]
        out_ref[j0 : j0 + step] = result.astype(bf16).reshape(step, residues, LANES)


MIB = 1 << 20
VMEM_BYTES = 67_043_328


def fast_shards(n, alignment, pair_rep, align_gain, align_offset, left_weight, right_weight, *layer_params):
    seq, residues, channels = alignment.shape
    lay = Layout(n, seq, residues, pair_rep.shape[0], left_weight.shape[1])
    f32, bf16 = jnp.float32, jnp.bfloat16
    me = lax.axis_index("row")
    place = jnp.stack([me // CORES, me % CORES]).astype(jnp.int32)
    sent = pl.pallas_call(
        functools.partial(send_kernel, lay),
        out_shape=[jax.ShapeDtypeStruct((lay.total(k), LANES), bf16) for k in range(lay.chips)],
        in_specs=[SMEM] + [VMEM] * 6,
        out_specs=[VMEM] * lay.chips,
        scratch_shapes=[
            pltpu.VMEM((channels // LANES, seq * residues, LANES), f32),
            pltpu.VMEM((seq * lay.proj, LANES), f32),
        ],
        compiler_params=pltpu.CompilerParams(vmem_limit_bytes=VMEM_BYTES - sum(map(lay.total, range(lay.chips))) * 2 * LANES - 150_000),
        name="send",
    )(
        place,
        alignment,
        pair_rep,
        align_gain.reshape(1, -1),
        align_offset.reshape(1, -1),
        left_weight.T,
        right_weight.T,
    )

    def permute(x, k):
        return lax.ppermute(x, "row", [(d, d ^ k) for d in range(n)])

    got = {k: permute(sent[k], CORES * k) if k else sent[0] for k in range(lay.chips)}
    relayed = {k: permute(got[k ^ 1][: lay.relayed], CORES) for k in range(lay.chips) if lay.pair_only(k)}
    operands, outers, pairs = [], [], []

    def take(x, k, core, outer, pair):
        if outer is not None:
            outers.append((len(operands), outer))
        if pair is not None:
            pairs.append((len(operands), pair, CORES * k + core))
        operands.append(x)

    for k in range(lay.chips):
        outer = None if lay.pair_only(k) else lay.right_at(k)
        take(got[k], k, 0, outer, lay.pair_at(k))
        take(permute(got[k], 1), k, 1, outer, lay.pair_at(k))
        if k in relayed:
            take(relayed[k], k, 0, lay.left, None)
            take(permute(relayed[k], 1), k, 1, lay.left, None)
    ow, ob, pg, ps, uw, ub, dw, db = layer_params
    rows_j = lay.rows
    return pl.pallas_call(
        functools.partial(update_kernel, lay, outers, pairs),
        out_shape=jax.ShapeDtypeStruct((rows_j, residues, LANES), bf16),
        in_specs=[SMEM] + [VMEM] * (len(operands) + 8),
        out_specs=VMEM,
        scratch_shapes=[
            pltpu.VMEM((lay.proj * lay.proj, rows_j * residues), bf16),
            pltpu.VMEM((rows_j, residues, LANES), f32),
        ],
        compiler_params=pltpu.CompilerParams(vmem_limit_bytes=16 * MIB),
        name="update",
    )(
        place,
        *operands,
        ow,
        ob.reshape(1, -1),
        pg.reshape(1, -1),
        ps.reshape(1, -1),
        uw,
        ub.reshape(1, -1),
        dw,
        db.reshape(1, -1),
    )


def fits(n, alignment, pair_rep, left_weight):
    seq, residues, _ = alignment.shape
    rows, _, width = pair_rep.shape
    return (
        n >= 8
        and n & (n - 1) == 0
        and seq == 8
        and rows == 8
        and residues == LANES
        and width == LANES
        and left_weight.shape[1] == 32
    )


def solution(mesh):
    n = mesh.shape["row"]

    def shards(alignment, pair_rep, align_gain, align_offset, left_weight, right_weight, *layer_params):
        if fits(n, alignment, pair_rep, left_weight):
            return fast_shards(n, alignment, pair_rep, align_gain, align_offset, left_weight, right_weight, *layer_params)
        return plain_shards(alignment, pair_rep, align_gain, align_offset, left_weight, right_weight, *layer_params)

    split = P(("group", "row"), None, None)
    return jax.shard_map(
        shards,
        mesh=mesh,
        in_specs=(split, split) + (P(),) * 12,
        out_specs=split,
        check_vma=False,
    )
```

profile of v0, /device:TPU:0, one launch (start us, length us, event | category | flops | bytes accessed | tf_op | source)
XLA Modules:
  0.0 38.3 jit_solution(1861982111134511110)
XLA Ops:
  0.0 0.7 %pad_add_fusion.place = s32[2]{0:T(128)} fusion(s32[1]{0:T(128)} %bitcast.1, s32[1]{0:T(128)} %bitcast), kind=kLoop, calls=%fused_computation | loop fusion | flops 2 | bytes 16 | tf_op jit(solution)/shard_map/stack | solution.py:240
  0.7 3.2 %send.1 = (bf16[416,128]{1,0:T(8,128)(2,1)}, bf16[416,128]{1,0:T(8,128)(2,1)}, bf16[416,128]{1,0:T(8,128)(2,1)}, bf16[416,128]{1,0:T(8,128)(2,1)}, bf16[448,128]...) custom-call(s32[2]{0:T(128)} %pad_add_fusion.place, ...), custom_call_target="tpu_custom_call" | custom-call | tf_op jit(solution)/shard_map/send/pallas_call | solution.py:241
  3.9 5.1 %collective-permute-start.9 = (bf16[128,128]{1,0:T(8,128)(2,1)}, bf16[128,128]{1,0:T(8,128)(2,1)S(1)}, u32[]{:S(2)}, u32[]{:S(2)}) collective-permute-start(bf16[128,128]{1,0:T(8,128)(2,1)} %get-tuple-element.18), channel_id=1, source_target_pairs={{0,10},{1,11},{2,8},{3,9},{4,14},{5,15},{6,12},{7,13},{8,2},{9,3},... | collective-permute-start | bytes 98312 | tf_op jit(solution)/shard_map/ppermute | solution.py:263
  8.9 1.3 %collective-permute-start.15 = (bf16[128,128]{1,0:T(8,128)(2,1)}, bf16[128,128]{1,0:T(8,128)(2,1)S(1)}, u32[]{:S(2)}, u32[]{:S(2)}) collective-permute-start(bf16[128,128]{1,0:T(8,128)(2,1)} %get-tuple-element.20), channel_id=1, source_target_pairs={{0,14},{1,15},{2,12},{3,13},{4,10},{5,11},{6,8},{7,9},{8,6},{9,7},... | collective-permute-start | bytes 98312 | tf_op jit(solution)/shard_map/ppermute | solution.py:263
  10.2 1.7 %collective-permute-start.7 = (bf16[448,128]{1,0:T(8,128)(2,1)}, bf16[448,128]{1,0:T(8,128)(2,1)S(1)}, u32[]{:S(2)}, u32[]{:S(2)}) collective-permute-start(bf16[448,128]{1,0:T(8,128)(2,1)} %get-tuple-element.17), channel_id=1, source_target_pairs={{0,8},{1,9},{2,10},{3,11},{4,12},{5,13},{6,14},{7,15},{8,0},{9,1},... | collective-permute-start | bytes 344072 | tf_op jit(solution)/shard_map/ppermute | solution.py:263
  11.9 4.1 %collective-permute-done.15.rest_16_ = bf16[128,128]{1,0:T(8,128)(2,1)S(1)} collective-permute-done((bf16[128,128]{1,0:T(8,128)(2,1)}, bf16[128,128]{1,0:T(8,128)(2,1)S(1)}, u32[]{:S(2)}, u32[]{:S(2)}) %collective-permute-start.15) | collective-permute-done | bytes 32800 | tf_op jit(solution)/shard_map/ppermute | solution.py:263
  16.0 1.5 %collective-permute-start.13 = (bf16[448,128]{1,0:T(8,128)(2,1)}, bf16[448,128]{1,0:T(8,128)(2,1)S(1)}, u32[]{:S(2)}, u32[]{:S(2)}) collective-permute-start(bf16[448,128]{1,0:T(8,128)(2,1)} %get-tuple-element.19), channel_id=1, source_target_pairs={{0,12},{1,13},{2,14},{3,15},{4,8},{5,9},{6,10},{7,11},{8,4},{9,5},... | collective-permute-start | bytes 344072 | tf_op jit(solution)/shard_map/ppermute | solution.py:263
  17.6 0.5 %collective-permute-start.1 = (bf16[416,128]{1,0:T(8,128)(2,1)}, bf16[416,128]{1,0:T(8,128)(2,1)S(1)}, u32[]{:S(2)}, u32[]{:S(2)}) collective-permute-start(bf16[416,128]{1,0:T(8,128)(2,1)} %get-tuple-element.14), channel_id=1, source_target_pairs={{0,2},{1,3},{2,0},{3,1},{4,6},{5,7},{6,4},{7,5},{8,10},{9,11},{10,... | collective-permute-start | bytes 319496 | tf_op jit(solution)/shard_map/ppermute | solution.py:263
  18.1 1.9 %collective-permute-start.3 = (bf16[416,128]{1,0:T(8,128)(2,1)}, bf16[416,128]{1,0:T(8,128)(2,1)S(1)}, u32[]{:S(2)}, u32[]{:S(2)}) collective-permute-start(bf16[416,128]{1,0:T(8,128)(2,1)} %get-tuple-element.15), channel_id=1, source_target_pairs={{0,4},{1,5},{2,6},{3,7},{4,0},{5,1},{6,2},{7,3},{8,12},{9,13},{10,... | collective-permute-start | bytes 319496 | tf_op jit(solution)/shard_map/ppermute | solution.py:263
  20.0 1.1 %collective-permute-start.5 = (bf16[416,128]{1,0:T(8,128)(2,1)}, bf16[416,128]{1,0:T(8,128)(2,1)S(1)}, u32[]{:S(2)}, u32[]{:S(2)}) collective-permute-start(bf16[416,128]{1,0:T(8,128)(2,1)} %get-tuple-element.16), channel_id=1, source_target_pairs={{0,6},{1,7},{2,4},{3,5},{4,2},{5,3},{6,0},{7,1},{8,14},{9,15},{10,... | collective-permute-start | bytes 319496 | tf_op jit(solution)/shard_map/ppermute | solution.py:263
  21.1 3.0 %collective-permute-done.13.rest_14_ = bf16[448,128]{1,0:T(8,128)(2,1)S(1)} collective-permute-done((bf16[448,128]{1,0:T(8,128)(2,1)}, bf16[448,128]{1,0:T(8,128)(2,1)S(1)}, u32[]{:S(2)}, u32[]{:S(2)}) %collective-permute-start.13) | collective-permute-done | bytes 114720 | tf_op jit(solution)/shard_map/ppermute | solution.py:263
  24.1 0.2 collective-permute-start.11
  24.3 1.9 %collective-permute-start.17 = (bf16[288,128]{1,0:T(8,128)(2,1)S(1)}, bf16[288,128]{1,0:T(8,128)(2,1)S(1)}, u32[]{:S(2)}, u32[]{:S(2)}) collective-permute-start(bf16[288,128]{1,0:T(8,128)(2,1)S(1)} %slice.9), channel_id=1, source_target_pairs={{0,2},{1,3},{2,0},{3,1},{4,6},{5,7},{6,4},{7,5},{8,10},{9,11},{10,... | collective-permute-start | bytes 221192 | tf_op jit(solution)/shard_map/ppermute | solution.py:263
  26.2 2.0 %collective-permute-done.5.rest_6_ = bf16[416,128]{1,0:T(8,128)(2,1)S(1)} collective-permute-done((bf16[416,128]{1,0:T(8,128)(2,1)}, bf16[416,128]{1,0:T(8,128)(2,1)S(1)}, u32[]{:S(2)}, u32[]{:S(2)}) %collective-permute-start.5) | collective-permute-done | bytes 106528 | tf_op jit(solution)/shard_map/ppermute | solution.py:263
  28.3 0.5 %collective-permute-start.8 = (bf16[448,128]{1,0:T(8,128)(2,1)S(1)}, bf16[448,128]{1,0:T(8,128)(2,1)S(1)}, u32[]{:S(2)}, u32[]{:S(2)}) collective-permute-start(bf16[448,128]{1,0:T(8,128)(2,1)S(1)} %collective-permute-done.7.rest_8_), channel_id=1, source_target_pairs={{0,1},{1,0},{2,3},{3,2},{4,5},{5,4},{6,7},{7,6},{8,9},{9,8},{10,11... | collective-permute-start | bytes 344072 | tf_op jit(solution)/shard_map/ppermute | solution.py:263
  28.8 1.1 %collective-permute-done.11.rest_12_ = bf16[288,128]{1,0:T(8,128)(2,1)S(1)} collective-permute-done((bf16[288,128]{1,0:T(8,128)(2,1)S(1)}, bf16[288,128]{1,0:T(8,128)(2,1)S(1)}, u32[]{:S(2)}, u32[]{:S(2)}) %collective-permute-start.11) | collective-permute-done | bytes 73760 | tf_op jit(solution)/shard_map/ppermute | solution.py:263
  29.8 1.4 %collective-permute-done.17.rest_18_ = bf16[288,128]{1,0:T(8,128)(2,1)S(1)} collective-permute-done((bf16[288,128]{1,0:T(8,128)(2,1)S(1)}, bf16[288,128]{1,0:T(8,128)(2,1)S(1)}, u32[]{:S(2)}, u32[]{:S(2)}) %collective-permute-start.17) | collective-permute-done | bytes 73760 | tf_op jit(solution)/shard_map/ppermute | solution.py:263
  31.3 0.5 %collective-permute-start.12 = (bf16[288,128]{1,0:T(8,128)(2,1)S(1)}, bf16[288,128]{1,0:T(8,128)(2,1)S(1)}, u32[]{:S(2)}, u32[]{:S(2)}) collective-permute-start(bf16[288,128]{1,0:T(8,128)(2,1)S(1)} %collective-permute-done.11.rest_12_), channel_id=1, source_target_pairs={{0,1},{1,0},{2,3},{3,2},{4,5},{5,4},{6,7},{7,6},{8,9},{9,8},{10,11... | collective-permute-start | bytes 221192 | tf_op jit(solution)/shard_map/ppermute | solution.py:263
  31.9 0.7 %collective-permute-done.6.rest_7_ = bf16[416,128]{1,0:T(8,128)(2,1)S(1)} collective-permute-done((bf16[416,128]{1,0:T(8,128)(2,1)S(1)}, bf16[416,128]{1,0:T(8,128)(2,1)S(1)}, u32[]{:S(2)}, u32[]{:S(2)}) %collective-permute-start.6) | collective-permute-done | bytes 106528 | tf_op jit(solution)/shard_map/ppermute | solution.py:263
  32.6 0.1 collective-permute-done.12.rest_13_
  32.7 0.4 collective-permute-done.18.rest_19_
  33.1 0.6 %copy-done.4 = f32[512]{0:T(512)S(1)} copy-done((f32[512]{0:T(512)S(1)}, f32[512]{0:T(512)}, u32[]{:S(2)}) %copy-start.4) | copy-done | bytes 2072
  33.8 0.9 %copy-done.3 = bf16[416,128]{1,0:T(8,128)(2,1)S(1)} copy-done((bf16[416,128]{1,0:T(8,128)(2,1)S(1)}, bf16[416,128]{1,0:T(8,128)(2,1)}, u32[]{:S(2)}) %copy-start.3) | copy-done | bytes 106520
  34.6 3.7 %update.1 = bf16[8,128,128]{2,1,0:T(8,128)(2,1)} custom-call(s32[2]{0:T(128)S(1)} %copy-done.5, bf16[416,128]{1,0:T(8,128)(2,1)S(1)} %copy-done.3, bf16[416,128]{1,0:T(8,128)(2,1)S(1)} %collective-permute-done.rest_1_, bf16[416,128]{1,0:T(8,128)(2,1)S(1)} %collective-permute-done.1.rest_2_, bf16[416,128]{1,0:T(8,128)(2,1)S(1)} %collective-permute-done.2.rest_3_, ...), custom_call_target="tpu_custom_call" | custom-call | tf_op jit(solution)/shard_map/update/pallas_call | solution.py:285
  (39 shorter events, 0.2 us)
Async XLA Ops:
  0.7 32.4 %copy-start.1 = (bf16[128,512]{1,0:T(8,128)(2,1)S(1)}, bf16[128,512]{1,0:T(8,128)(2,1)}, u32[]{:S(2)}) copy-start(bf16[128,512]{1,0:T(8,128)(2,1)} %rest_24_.1) | copy-start | bytes 393220
  0.7 32.4 %copy-start.2 = (bf16[512,128]{1,0:T(8,128)(2,1)S(1)}, bf16[512,128]{1,0:T(8,128)(2,1)}, u32[]{:S(2)}) copy-start(bf16[512,128]{1,0:T(8,128)(2,1)} %rest_26_.1) | copy-start | bytes 393220
  3.9 29.2 %copy-start = (bf16[1024,128]{1,0:T(8,128)(2,1)S(1)}, bf16[1024,128]{1,0:T(8,128)(2,1)}, u32[]{:S(2)}) copy-start(bf16[1024,128]{1,0:T(8,128)(2,1)} %rest_20_.1) | copy-start | bytes 786436
  3.9 8.1 %collective-permute-start.9 = (bf16[128,128]{1,0:T(8,128)(2,1)}, bf16[128,128]{1,0:T(8,128)(2,1)S(1)}, u32[]{:S(2)}, u32[]{:S(2)}) collective-permute-start(bf16[128,128]{1,0:T(8,128)(2,1)} %get-tuple-element.18), channel_id=1, source_target_pairs={{0,10},{1,11},{2,8},{3,9},{4,14},{5,15},{6,12},{7,13},{8,2},{9,3},... | collective-permute-start | bytes 98312 | tf_op jit(solution)/shard_map/ppermute | solution.py:263
  8.9 7.1 %collective-permute-start.15 = (bf16[128,128]{1,0:T(8,128)(2,1)}, bf16[128,128]{1,0:T(8,128)(2,1)S(1)}, u32[]{:S(2)}, u32[]{:S(2)}) collective-permute-start(bf16[128,128]{1,0:T(8,128)(2,1)} %get-tuple-element.20), channel_id=1, source_target_pairs={{0,14},{1,15},{2,12},{3,13},{4,10},{5,11},{6,8},{7,9},{8,6},{9,7},... | collective-permute-start | bytes 98312 | tf_op jit(solution)/shard_map/ppermute | solution.py:263
  10.2 10.8 %collective-permute-start.7 = (bf16[448,128]{1,0:T(8,128)(2,1)}, bf16[448,128]{1,0:T(8,128)(2,1)S(1)}, u32[]{:S(2)}, u32[]{:S(2)}) collective-permute-start(bf16[448,128]{1,0:T(8,128)(2,1)} %get-tuple-element.17), channel_id=1, source_target_pairs={{0,8},{1,9},{2,10},{3,11},{4,12},{5,13},{6,14},{7,15},{8,0},{9,1},... | collective-permute-start | bytes 344072 | tf_op jit(solution)/shard_map/ppermute | solution.py:263
  11.9 6.2 %collective-permute-start.10 = (bf16[128,128]{1,0:T(8,128)(2,1)S(1)}, bf16[128,128]{1,0:T(8,128)(2,1)S(1)}, u32[]{:S(2)}, u32[]{:S(2)}) collective-permute-start(bf16[128,128]{1,0:T(8,128)(2,1)S(1)} %collective-permute-done.9.rest_10_), channel_id=1, source_target_pairs={{0,1},{1,0},{2,3},{3,2},{4,5},{5,4},{6,7},{7,6},{8,9},{9,8},{10,11... | collective-permute-start | bytes 98312 | tf_op jit(solution)/shard_map/ppermute | solution.py:263
  16.0 4.0 %collective-permute-start.16 = (bf16[128,128]{1,0:T(8,128)(2,1)S(1)}, bf16[128,128]{1,0:T(8,128)(2,1)S(1)}, u32[]{:S(2)}, u32[]{:S(2)}) collective-permute-start(bf16[128,128]{1,0:T(8,128)(2,1)S(1)} %collective-permute-done.15.rest_16_), channel_id=1, source_target_pairs={{0,1},{1,0},{2,3},{3,2},{4,5},{5,4},{6,7},{7,6},{8,9},{9,8},{10,11... | collective-permute-start | bytes 98312 | tf_op jit(solution)/shard_map/ppermute | solution.py:263
  16.0 8.1 %collective-permute-start.13 = (bf16[448,128]{1,0:T(8,128)(2,1)}, bf16[448,128]{1,0:T(8,128)(2,1)S(1)}, u32[]{:S(2)}, u32[]{:S(2)}) collective-permute-start(bf16[448,128]{1,0:T(8,128)(2,1)} %get-tuple-element.19), channel_id=1, source_target_pairs={{0,12},{1,13},{2,14},{3,15},{4,8},{5,9},{6,10},{7,11},{8,4},{9,5},... | collective-permute-start | bytes 344072 | tf_op jit(solution)/shard_map/ppermute | solution.py:263
  17.6 6.7 %collective-permute-start.1 = (bf16[416,128]{1,0:T(8,128)(2,1)}, bf16[416,128]{1,0:T(8,128)(2,1)S(1)}, u32[]{:S(2)}, u32[]{:S(2)}) collective-permute-start(bf16[416,128]{1,0:T(8,128)(2,1)} %get-tuple-element.14), channel_id=1, source_target_pairs={{0,2},{1,3},{2,0},{3,1},{4,6},{5,7},{6,4},{7,5},{8,10},{9,11},{10,... | collective-permute-start | bytes 319496 | tf_op jit(solution)/shard_map/ppermute | solution.py:263
  18.1 8.1 %collective-permute-start.3 = (bf16[416,128]{1,0:T(8,128)(2,1)}, bf16[416,128]{1,0:T(8,128)(2,1)S(1)}, u32[]{:S(2)}, u32[]{:S(2)}) collective-permute-start(bf16[416,128]{1,0:T(8,128)(2,1)} %get-tuple-element.15), channel_id=1, source_target_pairs={{0,4},{1,5},{2,6},{3,7},{4,0},{5,1},{6,2},{7,3},{8,12},{9,13},{10,... | collective-permute-start | bytes 319496 | tf_op jit(solution)/shard_map/ppermute | solution.py:263
  20.0 8.3 %collective-permute-start.5 = (bf16[416,128]{1,0:T(8,128)(2,1)}, bf16[416,128]{1,0:T(8,128)(2,1)S(1)}, u32[]{:S(2)}, u32[]{:S(2)}) collective-permute-start(bf16[416,128]{1,0:T(8,128)(2,1)} %get-tuple-element.16), channel_id=1, source_target_pairs={{0,6},{1,7},{2,4},{3,5},{4,2},{5,3},{6,0},{7,1},{8,14},{9,15},{10,... | collective-permute-start | bytes 319496 | tf_op jit(solution)/shard_map/ppermute | solution.py:263
  21.1 7.2 %collective-permute-start = (bf16[416,128]{1,0:T(8,128)(2,1)}, bf16[416,128]{1,0:T(8,128)(2,1)S(1)}, u32[]{:S(2)}, u32[]{:S(2)}) collective-permute-start(bf16[416,128]{1,0:T(8,128)(2,1)} %get-tuple-element.13.rest_0_), channel_id=1, source_target_pairs={{0,1},{1,0},{2,3},{3,2},{4,5},{5,4},{6,7},{7,6},{8,9},{9,8},{10,11... | collective-permute-start | bytes 319496 | tf_op jit(solution)/shard_map/ppermute | solution.py:263
  24.1 5.7 %collective-permute-start.11 = (bf16[288,128]{1,0:T(8,128)(2,1)S(1)}, bf16[288,128]{1,0:T(8,128)(2,1)S(1)}, u32[]{:S(2)}, u32[]{:S(2)}) collective-permute-start(bf16[288,128]{1,0:T(8,128)(2,1)S(1)} %slice.8), channel_id=1, source_target_pairs={{0,2},{1,3},{2,0},{3,1},{4,6},{5,7},{6,4},{7,5},{8,10},{9,11},{10,... | collective-permute-start | bytes 221192 | tf_op jit(solution)/shard_map/ppermute | solution.py:263
  24.3 8.8 %copy-start.8 = (f32[128]{0:T(128)S(1)}, f32[128]{0:T(128)}, u32[]{:S(2)}) copy-start(f32[128]{0:T(128)} %param.23) | copy-start | bytes 1540
  24.3 8.8 %copy-start.9 = (f32[128]{0:T(128)S(1)}, f32[128]{0:T(128)}, u32[]{:S(2)}) copy-start(f32[128]{0:T(128)} %param.27) | copy-start | bytes 1540
  24.3 7.0 %collective-permute-start.17 = (bf16[288,128]{1,0:T(8,128)(2,1)S(1)}, bf16[288,128]{1,0:T(8,128)(2,1)S(1)}, u32[]{:S(2)}, u32[]{:S(2)}) collective-permute-start(bf16[288,128]{1,0:T(8,128)(2,1)S(1)} %slice.9), channel_id=1, source_target_pairs={{0,2},{1,3},{2,0},{3,1},{4,6},{5,7},{6,4},{7,5},{8,10},{9,11},{10,... | collective-permute-start | bytes 221192 | tf_op jit(solution)/shard_map/ppermute | solution.py:263
  26.2 5.1 %collective-permute-start.2 = (bf16[416,128]{1,0:T(8,128)(2,1)S(1)}, bf16[416,128]{1,0:T(8,128)(2,1)S(1)}, u32[]{:S(2)}, u32[]{:S(2)}) collective-permute-start(bf16[416,128]{1,0:T(8,128)(2,1)S(1)} %collective-permute-done.1.rest_2_), channel_id=1, source_target_pairs={{0,1},{1,0},{2,3},{3,2},{4,5},{5,4},{6,7},{7,6},{8,9},{9,8},{10,11... | collective-permute-start | bytes 319496 | tf_op jit(solution)/shard_map/ppermute | solution.py:263
  28.3 3.5 %collective-permute-start.4 = (bf16[416,128]{1,0:T(8,128)(2,1)S(1)}, bf16[416,128]{1,0:T(8,128)(2,1)S(1)}, u32[]{:S(2)}, u32[]{:S(2)}) collective-permute-start(bf16[416,128]{1,0:T(8,128)(2,1)S(1)} %collective-permute-done.3.rest_4_), channel_id=1, source_target_pairs={{0,1},{1,0},{2,3},{3,2},{4,5},{5,4},{6,7},{7,6},{8,9},{9,8},{10,11... | collective-permute-start | bytes 319496 | tf_op jit(solution)/shard_map/ppermute | solution.py:263
  28.3 4.3 %collective-permute-start.8 = (bf16[448,128]{1,0:T(8,128)(2,1)S(1)}, bf16[448,128]{1,0:T(8,128)(2,1)S(1)}, u32[]{:S(2)}, u32[]{:S(2)}) collective-permute-start(bf16[448,128]{1,0:T(8,128)(2,1)S(1)} %collective-permute-done.7.rest_8_), channel_id=1, source_target_pairs={{0,1},{1,0},{2,3},{3,2},{4,5},{5,4},{6,7},{7,6},{8,9},{9,8},{10,11... | collective-permute-start | bytes 344072 | tf_op jit(solution)/shard_map/ppermute | solution.py:263
  29.8 2.8 %collective-permute-start.14 = (bf16[448,128]{1,0:T(8,128)(2,1)S(1)}, bf16[448,128]{1,0:T(8,128)(2,1)S(1)}, u32[]{:S(2)}, u32[]{:S(2)}) collective-permute-start(bf16[448,128]{1,0:T(8,128)(2,1)S(1)} %collective-permute-done.13.rest_14_), channel_id=1, source_target_pairs={{0,1},{1,0},{2,3},{3,2},{4,5},{5,4},{6,7},{7,6},{8,9},{9,8},{10,11... | collective-permute-start | bytes 344072 | tf_op jit(solution)/shard_map/ppermute | solution.py:263
  31.3 1.3 %collective-permute-start.6 = (bf16[416,128]{1,0:T(8,128)(2,1)S(1)}, bf16[416,128]{1,0:T(8,128)(2,1)S(1)}, u32[]{:S(2)}, u32[]{:S(2)}) collective-permute-start(bf16[416,128]{1,0:T(8,128)(2,1)S(1)} %collective-permute-done.5.rest_6_), channel_id=1, source_target_pairs={{0,1},{1,0},{2,3},{3,2},{4,5},{5,4},{6,7},{7,6},{8,9},{9,8},{10,11... | collective-permute-start | bytes 319496 | tf_op jit(solution)/shard_map/ppermute | solution.py:263
  31.3 1.4 %collective-permute-start.12 = (bf16[288,128]{1,0:T(8,128)(2,1)S(1)}, bf16[288,128]{1,0:T(8,128)(2,1)S(1)}, u32[]{:S(2)}, u32[]{:S(2)}) collective-permute-start(bf16[288,128]{1,0:T(8,128)(2,1)S(1)} %collective-permute-done.11.rest_12_), channel_id=1, source_target_pairs={{0,1},{1,0},{2,3},{3,2},{4,5},{5,4},{6,7},{7,6},{8,9},{9,8},{10,11... | collective-permute-start | bytes 221192 | tf_op jit(solution)/shard_map/ppermute | solution.py:263
  31.8 1.3 %collective-permute-start.18 = (bf16[288,128]{1,0:T(8,128)(2,1)S(1)}, bf16[288,128]{1,0:T(8,128)(2,1)S(1)}, u32[]{:S(2)}, u32[]{:S(2)}) collective-permute-start(bf16[288,128]{1,0:T(8,128)(2,1)S(1)} %collective-permute-done.17.rest_18_), channel_id=1, source_target_pairs={{0,1},{1,0},{2,3},{3,2},{4,5},{5,4},{6,7},{7,6},{8,9},{9,8},{10,11... | collective-permute-start | bytes 221192 | tf_op jit(solution)/shard_map/ppermute | solution.py:263
  (5 other events, 3.6 us)
where the time goes:
time: 38.5 us; the launch traced here: 38.3 us
  starting transfers between devices  16.3 us (42%)
  waiting for transfers between devices  12.9 us (34%)
  Pallas kernels  6.9 us (18%)
  local copies, waits for them, and re-layouts  1.56 us (4%)
  other arithmetic  0.65 us (2%)
    ppermute x19, starting transfers between devices, permute(): return lax.ppermute(x, 'row', [(d, d ^ k) for d in range(n)])  16.3 us
    ppermute x19, waiting for transfers between devices, permute(): return lax.ppermute(x, 'row', [(d, d ^ k) for d in range(n)])  12.9 us
    pallas_call x1, Pallas kernels, fast_shards(): pl.pallas_call(functools.partial(update_kernel, lay, outers, pairs), out_...  3.7 us
    pallas_call x1, Pallas kernels, fast_shards(): pl.pallas_call(functools.partial(send_kernel, lay), out_shape=[jax.ShapeD...  3.2 us
    unnamed x20, local copies, waits for them, and re-layouts  1.55 us
  transfers between devices with their start and end apart: 19, of which 8 were waited for; matrix products, arithmetic and copies ran while one was open for 0% of the time, Pallas kernels for 0%

commit v1 on v0

--- a/solution.py
+++ b/solution.py
@@ -229,7 +229,31 @@
 
 
 MIB = 1 << 20
-VMEM_BYTES = 67_043_328
+
+
+def in_hbm(x):
+    return pltpu.with_memory_space_constraint(x, pltpu.HBM)
+
+
+def in_vmem(x):
+    return pltpu.with_memory_space_constraint(x, pltpu.VMEM)
+
+
+def load_kernel(*refs):
+    count = len(refs) // 2
+    for source, to in zip(refs[:count], refs[count:]):
+        to[...] = source[...]
+
+
+def load(arrays):
+    return pl.pallas_call(
+        load_kernel,
+        out_shape=[jax.ShapeDtypeStruct(a.shape, a.dtype) for a in arrays],
+        in_specs=[VMEM] * len(arrays),
+        out_specs=[VMEM] * len(arrays),
+        compiler_params=pltpu.CompilerParams(vmem_limit_bytes=4 * MIB),
+        name="load",
+    )(*[in_hbm(a) for a in arrays])
 
 
 def fast_shards(n, alignment, pair_rep, align_gain, align_offset, left_weight, right_weight, *layer_params):
@@ -247,16 +271,16 @@
             pltpu.VMEM((channels // LANES, seq * residues, LANES), f32),
             pltpu.VMEM((seq * lay.proj, LANES), f32),
         ],
-        compiler_params=pltpu.CompilerParams(vmem_limit_bytes=VMEM_BYTES - sum(map(lay.total, range(lay.chips))) * 2 * LANES - 150_000),
+        compiler_params=pltpu.CompilerParams(vmem_limit_bytes=8 * MIB),
         name="send",
     )(
         place,
-        alignment,
-        pair_rep,
-        align_gain.reshape(1, -1),
-        align_offset.reshape(1, -1),
-        left_weight.T,
-        right_weight.T,
+        in_hbm(alignment),
+        in_hbm(pair_rep),
+        in_hbm(align_gain.reshape(1, -1)),
+        in_hbm(align_offset.reshape(1, -1)),
+        in_hbm(left_weight.T),
+        in_hbm(right_weight.T),
     )
 
     def permute(x, k):
@@ -280,7 +304,7 @@
         if k in relayed:
             take(relayed[k], k, 0, lay.left, None)
             take(permute(relayed[k], 1), k, 1, lay.left, None)
-    ow, ob, pg, ps, uw, ub, dw, db = layer_params
+    params = load([p if p.ndim == 2 else p.reshape(1, -1) for p in layer_params])
     rows_j = lay.rows
     return pl.pallas_call(
         functools.partial(update_kernel, lay, outers, pairs),
@@ -295,15 +319,8 @@
         name="update",
     )(
         place,
-        *operands,
-        ow,
-        ob.reshape(1, -1),
-        pg.reshape(1, -1),
-        ps.reshape(1, -1),
-        uw,
-        ub.reshape(1, -1),
-        dw,
-        db.reshape(1, -1),
+        *[in_vmem(x) for x in operands],
+        *[in_vmem(x) for x in params],
     )
 
 

time: 38.5 us -> 35.1 us (0.912)
  waiting for transfers between devices: 12.9 us -> 11.3 us
  local copies, waits for them, and re-layouts: 1.56 us -> 0.01 us
  other arithmetic: 0.65 us -> 0.07 us
    ppermute x19, waiting for transfers between devices: 12.9 us -> 11.3 us  [permute(): return lax.ppermute(x, 'row', [(d, d ^ k) for d in range(n)])]
    unnamed x20 -> x0, local copies, waits for them, and re-layouts: 1.55 us -> none
    pallas_call x0 -> x1, Pallas kernels: none -> 1.15 us  [load(): pl.pallas_call(load_kernel, out_shape=[jax.ShapeDtypeStruct(a.shape, a.dt...]
    pallas_call x1, Pallas kernels: 3.2 us -> 2.37 us  [fast_shards(): pl.pallas_call(functools.partial(send_kernel, lay), out_shape=[jax.ShapeD...]
    another operation x1, other arithmetic: 0.65 us -> 0.07 us  [fast_shards(): place = jnp.stack([me // CORES, me % CORES]).astype(jnp.int32)]
  transfers between devices with their start and end apart: 19 -> 19, of which waited for: 8 -> 5; matrix products, arithmetic and copies ran while one was open for 0% -> 0% of each run, Pallas kernels for 0% -> 3%
where the time goes in v1:
time: 35.1 us; the launch traced here: 35 us
  starting transfers between devices  16.3 us (46%)
  waiting for transfers between devices  11.3 us (32%)
  Pallas kernels  7.26 us (21%)
    ppermute x19, starting transfers between devices, permute(): return lax.ppermute(x, 'row', [(d, d ^ k) for d in range(n)])  16.3 us
    ppermute x19, waiting for transfers between devices, permute(): return lax.ppermute(x, 'row', [(d, d ^ k) for d in range(n)])  11.3 us
    pallas_call x1, Pallas kernels, fast_shards(): pl.pallas_call(functools.partial(update_kernel, lay, outers, pairs), out_...  3.73 us
    pallas_call x1, Pallas kernels, fast_shards(): pl.pallas_call(functools.partial(send_kernel, lay), out_shape=[jax.ShapeD...  2.37 us
    pallas_call x1, Pallas kernels, load(): pl.pallas_call(load_kernel, out_shape=[jax.ShapeDtypeStruct(a.shape, a.dt...  1.15 us
  transfers between devices with their start and end apart: 19, of which 5 were waited for; matrix products, arithmetic and copies ran while one was open for 0% of the time, Pallas kernels for 3%

profile of v1, /device:TPU:0, one launch (start us, length us, event | category | flops | bytes accessed | tf_op | source)
XLA Modules:
  0.0 35.0 jit_solution(10095414879817973726)
XLA Ops:
  0.0 0.1 pad_add_fusion.place
  0.1 2.4 %send.1 = (bf16[416,128]{1,0:T(8,128)(2,1)S(1)}, bf16[416,128]{1,0:T(8,128)(2,1)S(1)}, bf16[416,128]{1,0:T(8,128)(2,1)S(1)}, bf16[416,128]{1,0:T(8,128)(2,1)S(1)...) custom-call(s32[2]{0:T(128)S(1)} %pad_add_fusion.place, ...), custom_call_target="tpu_custom_call" | custom-call | tf_op jit(solution)/shard_map/send/pallas_call | solution.py:265
  2.5 5.1 %collective-permute-start.9 = (bf16[128,128]{1,0:T(8,128)(2,1)S(1)}, bf16[128,128]{1,0:T(8,128)(2,1)S(1)}, u32[]{:S(2)}, u32[]{:S(2)}) collective-permute-start(bf16[128,128]{1,0:T(8,128)(2,1)S(1)} %get-tuple-element.26), channel_id=1, source_target_pairs={{0,10},{1,11},{2,8},{3,9},{4,14},{5,15},{6,12},{7,13},{8,2},{9,3},... | collective-permute-start | bytes 98312 | tf_op jit(solution)/shard_map/ppermute | solution.py:287
  7.5 1.3 %collective-permute-start.15 = (bf16[128,128]{1,0:T(8,128)(2,1)S(1)}, bf16[128,128]{1,0:T(8,128)(2,1)S(1)}, u32[]{:S(2)}, u32[]{:S(2)}) collective-permute-start(bf16[128,128]{1,0:T(8,128)(2,1)S(1)} %get-tuple-element.28), channel_id=1, source_target_pairs={{0,14},{1,15},{2,12},{3,13},{4,10},{5,11},{6,8},{7,9},{8,6},{9,7},... | collective-permute-start | bytes 98312 | tf_op jit(solution)/shard_map/ppermute | solution.py:287
  8.8 1.7 %collective-permute-start.7 = (bf16[448,128]{1,0:T(8,128)(2,1)S(1)}, bf16[448,128]{1,0:T(8,128)(2,1)S(1)}, u32[]{:S(2)}, u32[]{:S(2)}) collective-permute-start(bf16[448,128]{1,0:T(8,128)(2,1)S(1)} %get-tuple-element.25), channel_id=1, source_target_pairs={{0,8},{1,9},{2,10},{3,11},{4,12},{5,13},{6,14},{7,15},{8,0},{9,1},... | collective-permute-start | bytes 344072 | tf_op jit(solution)/shard_map/ppermute | solution.py:287
  10.5 3.9 %collective-permute-done.15.rest_16_ = bf16[128,128]{1,0:T(8,128)(2,1)S(1)} collective-permute-done((bf16[128,128]{1,0:T(8,128)(2,1)S(1)}, bf16[128,128]{1,0:T(8,128)(2,1)S(1)}, u32[]{:S(2)}, u32[]{:S(2)}) %collective-permute-start.15) | collective-permute-done | bytes 32800 | tf_op jit(solution)/shard_map/ppermute | solution.py:287
  14.4 1.5 %collective-permute-start.13 = (bf16[448,128]{1,0:T(8,128)(2,1)S(1)}, bf16[448,128]{1,0:T(8,128)(2,1)S(1)}, u32[]{:S(2)}, u32[]{:S(2)}) collective-permute-start(bf16[448,128]{1,0:T(8,128)(2,1)S(1)} %get-tuple-element.27), channel_id=1, source_target_pairs={{0,12},{1,13},{2,14},{3,15},{4,8},{5,9},{6,10},{7,11},{8,4},{9,5},... | collective-permute-start | bytes 344072 | tf_op jit(solution)/shard_map/ppermute | solution.py:287
  16.0 0.5 %collective-permute-start.1 = (bf16[416,128]{1,0:T(8,128)(2,1)S(1)}, bf16[416,128]{1,0:T(8,128)(2,1)S(1)}, u32[]{:S(2)}, u32[]{:S(2)}) collective-permute-start(bf16[416,128]{1,0:T(8,128)(2,1)S(1)} %get-tuple-element.22), channel_id=1, source_target_pairs={{0,2},{1,3},{2,0},{3,1},{4,6},{5,7},{6,4},{7,5},{8,10},{9,11},{10,... | collective-permute-start | bytes 319496 | tf_op jit(solution)/shard_map/ppermute | solution.py:287
  16.5 0.0 collective-permute-done.10.rest_11_
  16.5 1.9 %collective-permute-start.3 = (bf16[416,128]{1,0:T(8,128)(2,1)S(1)}, bf16[416,128]{1,0:T(8,128)(2,1)S(1)}, u32[]{:S(2)}, u32[]{:S(2)}) collective-permute-start(bf16[416,128]{1,0:T(8,128)(2,1)S(1)} %get-tuple-element.23), channel_id=1, source_target_pairs={{0,4},{1,5},{2,6},{3,7},{4,0},{5,1},{6,2},{7,3},{8,12},{9,13},{10,... | collective-permute-start | bytes 319496 | tf_op jit(solution)/shard_map/ppermute | solution.py:287
  18.4 0.0 collective-permute-done.16.rest_17_
  18.4 1.1 %collective-permute-start.5 = (bf16[416,128]{1,0:T(8,128)(2,1)S(1)}, bf16[416,128]{1,0:T(8,128)(2,1)S(1)}, u32[]{:S(2)}, u32[]{:S(2)}) collective-permute-start(bf16[416,128]{1,0:T(8,128)(2,1)S(1)} %get-tuple-element.24), channel_id=1, source_target_pairs={{0,6},{1,7},{2,4},{3,5},{4,2},{5,3},{6,0},{7,1},{8,14},{9,15},{10,... | collective-permute-start | bytes 319496 | tf_op jit(solution)/shard_map/ppermute | solution.py:287
  19.5 2.8 %collective-permute-done.13.rest_14_ = bf16[448,128]{1,0:T(8,128)(2,1)S(1)} collective-permute-done((bf16[448,128]{1,0:T(8,128)(2,1)S(1)}, bf16[448,128]{1,0:T(8,128)(2,1)S(1)}, u32[]{:S(2)}, u32[]{:S(2)}) %collective-permute-start.13) | collective-permute-done | bytes 114720 | tf_op jit(solution)/shard_map/ppermute | solution.py:287
  22.3 0.2 collective-permute-start.11
  22.4 0.0 collective-permute-done.1.rest_2_
  22.5 1.9 %collective-permute-start.17 = (bf16[288,128]{1,0:T(8,128)(2,1)S(1)}, bf16[288,128]{1,0:T(8,128)(2,1)S(1)}, u32[]{:S(2)}, u32[]{:S(2)}) collective-permute-start(bf16[288,128]{1,0:T(8,128)(2,1)S(1)} %slice.9), channel_id=1, source_target_pairs={{0,2},{1,3},{2,0},{3,1},{4,6},{5,7},{6,4},{7,5},{8,10},{9,11},{10,... | collective-permute-start | bytes 221192 | tf_op jit(solution)/shard_map/ppermute | solution.py:287
  24.4 2.0 %collective-permute-done.5.rest_6_ = bf16[416,128]{1,0:T(8,128)(2,1)S(1)} collective-permute-done((bf16[416,128]{1,0:T(8,128)(2,1)S(1)}, bf16[416,128]{1,0:T(8,128)(2,1)S(1)}, u32[]{:S(2)}, u32[]{:S(2)}) %collective-permute-start.5) | collective-permute-done | bytes 106528 | tf_op jit(solution)/shard_map/ppermute | solution.py:287
  26.5 0.5 %collective-permute-start.8 = (bf16[448,128]{1,0:T(8,128)(2,1)S(1)}, bf16[448,128]{1,0:T(8,128)(2,1)S(1)}, u32[]{:S(2)}, u32[]{:S(2)}) collective-permute-start(bf16[448,128]{1,0:T(8,128)(2,1)S(1)} %collective-permute-done.7.rest_8_), channel_id=1, source_target_pairs={{0,1},{1,0},{2,3},{3,2},{4,5},{5,4},{6,7},{7,6},{8,9},{9,8},{10,11... | collective-permute-start | bytes 344072 | tf_op jit(solution)/shard_map/ppermute | solution.py:287
  27.0 1.1 %collective-permute-done.11.rest_12_ = bf16[288,128]{1,0:T(8,128)(2,1)S(1)} collective-permute-done((bf16[288,128]{1,0:T(8,128)(2,1)S(1)}, bf16[288,128]{1,0:T(8,128)(2,1)S(1)}, u32[]{:S(2)}, u32[]{:S(2)}) %collective-permute-start.11) | collective-permute-done | bytes 73760 | tf_op jit(solution)/shard_map/ppermute | solution.py:287
  28.0 1.4 %collective-permute-done.17.rest_18_ = bf16[288,128]{1,0:T(8,128)(2,1)S(1)} collective-permute-done((bf16[288,128]{1,0:T(8,128)(2,1)S(1)}, bf16[288,128]{1,0:T(8,128)(2,1)S(1)}, u32[]{:S(2)}, u32[]{:S(2)}) %collective-permute-start.17) | collective-permute-done | bytes 73760 | tf_op jit(solution)/shard_map/ppermute | solution.py:287
  29.5 0.5 %collective-permute-start.12 = (bf16[288,128]{1,0:T(8,128)(2,1)S(1)}, bf16[288,128]{1,0:T(8,128)(2,1)S(1)}, u32[]{:S(2)}, u32[]{:S(2)}) collective-permute-start(bf16[288,128]{1,0:T(8,128)(2,1)S(1)} %collective-permute-done.11.rest_12_), channel_id=1, source_target_pairs={{0,1},{1,0},{2,3},{3,2},{4,5},{5,4},{6,7},{7,6},{8,9},{9,8},{10,11... | collective-permute-start | bytes 221192 | tf_op jit(solution)/shard_map/ppermute | solution.py:287
  30.0 0.1 collective-permute-start.18
  30.0 1.1 %load.1 = (bf16[1024,128]{1,0:T(8,128)(2,1)S(1)}, f32[1,128]{1,0:T(1,128)S(1)}, f32[1,128]{1,0:T(1,128)S(1)}, f32[1,128]{1,0:T(1,128)S(1)}, bf16[128,512]{1,0:T(...) custom-call(bf16[1024,128]{1,0:T(8,128)(2,1)} %refs_0_.1, ...), custom_call_target="tpu_custom_call" | custom-call | tf_op jit(solution)/shard_map/load/pallas_call | solution.py:249
  31.2 3.7 %update.1 = bf16[8,128,128]{2,1,0:T(8,128)(2,1)} custom-call(s32[2]{0:T(128)S(1)} %pad_add_fusion.place, bf16[416,128]{1,0:T(8,128)(2,1)S(1)} %get-tuple-element.21.rest_0_, bf16[416,128]{1,0:T(8,128)(2,1)S(1)} %collective-permute-done.rest_1_, bf16[416,128]{1,0:T(8,128)(2,1)S(1)} %collective-permute-done.1.rest_2_, ...), custom_call_target="tpu_custom_call" | custom-call | tf_op jit(solution)/shard_map/update/pallas_call | solution.py:309
  (20 shorter events, 0.1 us)
Async XLA Ops:
  2.5 8.1 %collective-permute-start.9 = (bf16[128,128]{1,0:T(8,128)(2,1)S(1)}, bf16[128,128]{1,0:T(8,128)(2,1)S(1)}, u32[]{:S(2)}, u32[]{:S(2)}) collective-permute-start(bf16[128,128]{1,0:T(8,128)(2,1)S(1)} %get-tuple-element.26), channel_id=1, source_target_pairs={{0,10},{1,11},{2,8},{3,9},{4,14},{5,15},{6,12},{7,13},{8,2},{9,3},... | collective-permute-start | bytes 98312 | tf_op jit(solution)/shard_map/ppermute | solution.py:287
  7.5 6.9 %collective-permute-start.15 = (bf16[128,128]{1,0:T(8,128)(2,1)S(1)}, bf16[128,128]{1,0:T(8,128)(2,1)S(1)}, u32[]{:S(2)}, u32[]{:S(2)}) collective-permute-start(bf16[128,128]{1,0:T(8,128)(2,1)S(1)} %get-tuple-element.28), channel_id=1, source_target_pairs={{0,14},{1,15},{2,12},{3,13},{4,10},{5,11},{6,8},{7,9},{8,6},{9,7},... | collective-permute-start | bytes 98312 | tf_op jit(solution)/shard_map/ppermute | solution.py:287
  8.8 10.6 %collective-permute-start.7 = (bf16[448,128]{1,0:T(8,128)(2,1)S(1)}, bf16[448,128]{1,0:T(8,128)(2,1)S(1)}, u32[]{:S(2)}, u32[]{:S(2)}) collective-permute-start(bf16[448,128]{1,0:T(8,128)(2,1)S(1)} %get-tuple-element.25), channel_id=1, source_target_pairs={{0,8},{1,9},{2,10},{3,11},{4,12},{5,13},{6,14},{7,15},{8,0},{9,1},... | collective-permute-start | bytes 344072 | tf_op jit(solution)/shard_map/ppermute | solution.py:287
  10.5 5.9 %collective-permute-start.10 = (bf16[128,128]{1,0:T(8,128)(2,1)S(1)}, bf16[128,128]{1,0:T(8,128)(2,1)S(1)}, u32[]{:S(2)}, u32[]{:S(2)}) collective-permute-start(bf16[128,128]{1,0:T(8,128)(2,1)S(1)} %collective-permute-done.9.rest_10_), channel_id=1, source_target_pairs={{0,1},{1,0},{2,3},{3,2},{4,5},{5,4},{6,7},{7,6},{8,9},{9,8},{10,11... | collective-permute-start | bytes 98312 | tf_op jit(solution)/shard_map/ppermute | solution.py:287
  14.4 4.0 %collective-permute-start.16 = (bf16[128,128]{1,0:T(8,128)(2,1)S(1)}, bf16[128,128]{1,0:T(8,128)(2,1)S(1)}, u32[]{:S(2)}, u32[]{:S(2)}) collective-permute-start(bf16[128,128]{1,0:T(8,128)(2,1)S(1)} %collective-permute-done.15.rest_16_), channel_id=1, source_target_pairs={{0,1},{1,0},{2,3},{3,2},{4,5},{5,4},{6,7},{7,6},{8,9},{9,8},{10,11... | collective-permute-start | bytes 98312 | tf_op jit(solution)/shard_map/ppermute | solution.py:287
  14.4 7.9 %collective-permute-start.13 = (bf16[448,128]{1,0:T(8,128)(2,1)S(1)}, bf16[448,128]{1,0:T(8,128)(2,1)S(1)}, u32[]{:S(2)}, u32[]{:S(2)}) collective-permute-start(bf16[448,128]{1,0:T(8,128)(2,1)S(1)} %get-tuple-element.27), channel_id=1, source_target_pairs={{0,12},{1,13},{2,14},{3,15},{4,8},{5,9},{6,10},{7,11},{8,4},{9,5},... | collective-permute-start | bytes 344072 | tf_op jit(solution)/shard_map/ppermute | solution.py:287
  16.0 6.5 %collective-permute-start.1 = (bf16[416,128]{1,0:T(8,128)(2,1)S(1)}, bf16[416,128]{1,0:T(8,128)(2,1)S(1)}, u32[]{:S(2)}, u32[]{:S(2)}) collective-permute-start(bf16[416,128]{1,0:T(8,128)(2,1)S(1)} %get-tuple-element.22), channel_id=1, source_target_pairs={{0,2},{1,3},{2,0},{3,1},{4,6},{5,7},{6,4},{7,5},{8,10},{9,11},{10,... | collective-permute-start | bytes 319496 | tf_op jit(solution)/shard_map/ppermute | solution.py:287
  16.5 7.9 %collective-permute-start.3 = (bf16[416,128]{1,0:T(8,128)(2,1)S(1)}, bf16[416,128]{1,0:T(8,128)(2,1)S(1)}, u32[]{:S(2)}, u32[]{:S(2)}) collective-permute-start(bf16[416,128]{1,0:T(8,128)(2,1)S(1)} %get-tuple-element.23), channel_id=1, source_target_pairs={{0,4},{1,5},{2,6},{3,7},{4,0},{5,1},{6,2},{7,3},{8,12},{9,13},{10,... | collective-permute-start | bytes 319496 | tf_op jit(solution)/shard_map/ppermute | solution.py:287
  18.4 8.0 %collective-permute-start.5 = (bf16[416,128]{1,0:T(8,128)(2,1)S(1)}, bf16[416,128]{1,0:T(8,128)(2,1)S(1)}, u32[]{:S(2)}, u32[]{:S(2)}) collective-permute-start(bf16[416,128]{1,0:T(8,128)(2,1)S(1)} %get-tuple-element.24), channel_id=1, source_target_pairs={{0,6},{1,7},{2,4},{3,5},{4,2},{5,3},{6,0},{7,1},{8,14},{9,15},{10,... | collective-permute-start | bytes 319496 | tf_op jit(solution)/shard_map/ppermute | solution.py:287
  19.5 7.0 %collective-permute-start = (bf16[416,128]{1,0:T(8,128)(2,1)S(1)}, bf16[416,128]{1,0:T(8,128)(2,1)S(1)}, u32[]{:S(2)}, u32[]{:S(2)}) collective-permute-start(bf16[416,128]{1,0:T(8,128)(2,1)S(1)} %get-tuple-element.21.rest_0_), channel_id=1, source_target_pairs={{0,1},{1,0},{2,3},{3,2},{4,5},{5,4},{6,7},{7,6},{8,9},{9,8},{10,11... | collective-permute-start | bytes 319496 | tf_op jit(solution)/shard_map/ppermute | solution.py:287
  22.3 5.7 %collective-permute-start.11 = (bf16[288,128]{1,0:T(8,128)(2,1)S(1)}, bf16[288,128]{1,0:T(8,128)(2,1)S(1)}, u32[]{:S(2)}, u32[]{:S(2)}) collective-permute-start(bf16[288,128]{1,0:T(8,128)(2,1)S(1)} %slice.8), channel_id=1, source_target_pairs={{0,2},{1,3},{2,0},{3,1},{4,6},{5,7},{6,4},{7,5},{8,10},{9,11},{10,... | collective-permute-start | bytes 221192 | tf_op jit(solution)/shard_map/ppermute | solution.py:287
  22.5 7.0 %collective-permute-start.17 = (bf16[288,128]{1,0:T(8,128)(2,1)S(1)}, bf16[288,128]{1,0:T(8,128)(2,1)S(1)}, u32[]{:S(2)}, u32[]{:S(2)}) collective-permute-start(bf16[288,128]{1,0:T(8,128)(2,1)S(1)} %slice.9), channel_id=1, source_target_pairs={{0,2},{1,3},{2,0},{3,1},{4,6},{5,7},{6,4},{7,5},{8,10},{9,11},{10,... | collective-permute-start | bytes 221192 | tf_op jit(solution)/shard_map/ppermute | solution.py:287
  24.4 5.1 %collective-permute-start.2 = (bf16[416,128]{1,0:T(8,128)(2,1)S(1)}, bf16[416,128]{1,0:T(8,128)(2,1)S(1)}, u32[]{:S(2)}, u32[]{:S(2)}) collective-permute-start(bf16[416,128]{1,0:T(8,128)(2,1)S(1)} %collective-permute-done.1.rest_2_), channel_id=1, source_target_pairs={{0,1},{1,0},{2,3},{3,2},{4,5},{5,4},{6,7},{7,6},{8,9},{9,8},{10,11... | collective-permute-start | bytes 319496 | tf_op jit(solution)/shard_map/ppermute | solution.py:287
  26.4 3.5 %collective-permute-start.4 = (bf16[416,128]{1,0:T(8,128)(2,1)S(1)}, bf16[416,128]{1,0:T(8,128)(2,1)S(1)}, u32[]{:S(2)}, u32[]{:S(2)}) collective-permute-start(bf16[416,128]{1,0:T(8,128)(2,1)S(1)} %collective-permute-done.3.rest_4_), channel_id=1, source_target_pairs={{0,1},{1,0},{2,3},{3,2},{4,5},{5,4},{6,7},{7,6},{8,9},{9,8},{10,11... | collective-permute-start | bytes 319496 | tf_op jit(solution)/shard_map/ppermute | solution.py:287
  26.5 4.8 %collective-permute-start.8 = (bf16[448,128]{1,0:T(8,128)(2,1)S(1)}, bf16[448,128]{1,0:T(8,128)(2,1)S(1)}, u32[]{:S(2)}, u32[]{:S(2)}) collective-permute-start(bf16[448,128]{1,0:T(8,128)(2,1)S(1)} %collective-permute-done.7.rest_8_), channel_id=1, source_target_pairs={{0,1},{1,0},{2,3},{3,2},{4,5},{5,4},{6,7},{7,6},{8,9},{9,8},{10,11... | collective-permute-start | bytes 344072 | tf_op jit(solution)/shard_map/ppermute | solution.py:287
  28.0 3.2 %collective-permute-start.14 = (bf16[448,128]{1,0:T(8,128)(2,1)S(1)}, bf16[448,128]{1,0:T(8,128)(2,1)S(1)}, u32[]{:S(2)}, u32[]{:S(2)}) collective-permute-start(bf16[448,128]{1,0:T(8,128)(2,1)S(1)} %collective-permute-done.13.rest_14_), channel_id=1, source_target_pairs={{0,1},{1,0},{2,3},{3,2},{4,5},{5,4},{6,7},{7,6},{8,9},{9,8},{10,11... | collective-permute-start | bytes 344072 | tf_op jit(solution)/shard_map/ppermute | solution.py:287
  29.5 1.7 %collective-permute-start.6 = (bf16[416,128]{1,0:T(8,128)(2,1)S(1)}, bf16[416,128]{1,0:T(8,128)(2,1)S(1)}, u32[]{:S(2)}, u32[]{:S(2)}) collective-permute-start(bf16[416,128]{1,0:T(8,128)(2,1)S(1)} %collective-permute-done.5.rest_6_), channel_id=1, source_target_pairs={{0,1},{1,0},{2,3},{3,2},{4,5},{5,4},{6,7},{7,6},{8,9},{9,8},{10,11... | collective-permute-start | bytes 319496 | tf_op jit(solution)/shard_map/ppermute | solution.py:287
  29.5 1.8 %collective-permute-start.12 = (bf16[288,128]{1,0:T(8,128)(2,1)S(1)}, bf16[288,128]{1,0:T(8,128)(2,1)S(1)}, u32[]{:S(2)}, u32[]{:S(2)}) collective-permute-start(bf16[288,128]{1,0:T(8,128)(2,1)S(1)} %collective-permute-done.11.rest_12_), channel_id=1, source_target_pairs={{0,1},{1,0},{2,3},{3,2},{4,5},{5,4},{6,7},{7,6},{8,9},{9,8},{10,11... | collective-permute-start | bytes 221192 | tf_op jit(solution)/shard_map/ppermute | solution.py:287
  30.0 1.3 %collective-permute-start.18 = (bf16[288,128]{1,0:T(8,128)(2,1)S(1)}, bf16[288,128]{1,0:T(8,128)(2,1)S(1)}, u32[]{:S(2)}, u32[]{:S(2)}) collective-permute-start(bf16[288,128]{1,0:T(8,128)(2,1)S(1)} %collective-permute-done.17.rest_18_), channel_id=1, source_target_pairs={{0,1},{1,0},{2,3},{3,2},{4,5},{5,4},{6,7},{7,6},{8,9},{9,8},{10,11... | collective-permute-start | bytes 221192 | tf_op jit(solution)/shard_map/ppermute | solution.py:287
